TPU v7x, 256 devices: a whole 4x4x8 slice. The times are simulated.
256 devices in a mesh: dp: 16 (over x_lo, y, core), mp: 8 (over z), side: 2 (over x_hi).
Axes of the slice: x: 4 (x_hi: 2, x_lo: 2; x = x_hi * 2 + x_lo), y: 4, z: 8, core: 2. Of those that a mesh axis runs over, the one named last changes fastest.
Arguments:
- tokens: bfloat16 [4096, 3072], P('dp', 'mp'), may hold values from -6 to 6
- up_weight: bfloat16 [2, 3072, 6144], P('side', 'dp', 'mp'), may hold values from -0.109375 to 0.109375
- down_weight: bfloat16 [2, 6144, 3072], P('side', 'mp', 'dp'), may hold values from -0.078125 to 0.078125
- mod_table: float32 [2, 50, 3, 3072], P('side'), may hold values from -3 to 3
- timesteps: int32 [16], P('dp'), may hold values from 0 to 49
- valid_counts: int32 [16], replicated, may hold values from 64 to 256, as said below
Outputs:
- block_out: bfloat16 [2, 4096, 3072], P('side', 'dp', 'mp')
- up_grads: float32 [3072, 6144], P(('dp', 'side'), 'mp')
- down_grads: float32 [6144, 3072], P('mp', ('dp', 'side'))
Inputs may be any that keep to these rules, and one draw needn't show every extreme that they name: `valid_counts`: every image has at least 64 valid tokens, and in every draw some image has all 256 valid.
All inputs are finite; a program needn't handle non-finite values.
Results may differ from a plain program's by a relative error of at most 0.018.
Values may be sent and summed in bfloat16 or wider, within the bound.
A program may use at most 64 MiB of HBM per device.

v0:
```python
import jax
import jax.numpy as jnp
from jax import lax
from jax.sharding import PartitionSpec as P


def passed_along(x, axis, by):
    peers = lax.axis_size(axis)
    pairs = [(i, i + by) for i in range(peers) if 0 <= i + by < peers]
    return lax.ppermute(x, axis, pairs)


def gelu_tanh(values):
    return jax.nn.gelu(values, approximate=True)


def shards(tokens, up_weight, down_weight, mod_table, timesteps, valid_counts):
    gathered = lax.all_gather(tokens, "mp", axis=1, tiled=True)
    width = gathered.shape[1]
    shard_width = tokens.shape[1]
    mp_offset = lax.axis_index("mp") * shard_width
    is_student = lax.axis_index("side") == 1
    wide = gathered.astype(jnp.float32)
    average = jnp.mean(wide, axis=-1, keepdims=True)
    centred = wide - average
    variance = jnp.mean(centred * centred, axis=-1, keepdims=True)
    scaled = centred * lax.rsqrt(variance + 1e-06)
    plan = mod_table.shape[1]
    one_hot = (jnp.arange(plan, dtype=jnp.int32)[None, :] == timesteps[0]).astype(jnp.float32)
    modulation = jnp.dot(
        one_hot,
        mod_table[0].reshape(plan, 3 * width),
        precision=lax.Precision.HIGHEST,
        preferred_element_type=jnp.float32,
    ).reshape(3, width)
    normed = (scaled * (1.0 + modulation[1]) + modulation[0]).astype(jnp.bfloat16)
    gate_row = modulation[2]
    hidden_pre = jnp.dot(
        normed,
        lax.all_gather(up_weight[0], "dp", axis=0, tiled=True),
        preferred_element_type=jnp.float32,
    )
    hidden_act = gelu_tanh(hidden_pre).astype(jnp.bfloat16)
    down_full = lax.all_gather(down_weight[0], "dp", axis=1, tiled=True)
    partial_value = jnp.dot(hidden_act, down_full, preferred_element_type=jnp.float32)
    positions = jnp.arange(normed.shape[0], dtype=jnp.int32)
    own_count = lax.dynamic_index_in_dim(valid_counts, lax.axis_index("dp"), 0, keepdims=False)
    valid_col = (positions < own_count).astype(jnp.float32)[:, None]
    valid_total = jnp.sum(valid_counts).astype(jnp.float32)
    mixed = lax.psum(partial_value.astype(jnp.bfloat16), "mp").astype(jnp.float32)
    out_full = (wide + gate_row * mixed).astype(jnp.bfloat16)
    out_local = lax.dynamic_slice_in_dim(out_full, mp_offset, shard_width, 1)
    other_full = passed_along(out_full, "side", 1)
    differ = out_full.astype(jnp.float32) - other_full.astype(jnp.float32)
    grad_out = (gate_row * differ * valid_col / jnp.sqrt(valid_total)).astype(jnp.bfloat16)

    def backprop():
        grad_act = lax.dot_general(
            grad_out, down_full, (((1,), (1,)), ((), ())), preferred_element_type=jnp.float32
        )
        unused, pullback = jax.vjp(gelu_tanh, hidden_pre)
        return pullback(grad_act)[0].astype(jnp.bfloat16)

    def no_backprop():
        return jnp.zeros(hidden_pre.shape, jnp.bfloat16)

    grad_pre = lax.cond(is_student, backprop, no_backprop)
    ff_width = hidden_act.shape[1]

    def product():
        return lax.dot_general(
            normed, grad_pre, (((0,), (0,)), ((), ())), preferred_element_type=jnp.float32
        )

    def nothing():
        return jnp.zeros(
            (width // lax.axis_size(("dp", "side")) * lax.axis_size(("dp", "side")), ff_width),
            jnp.float32,
        )

    up_share = lax.psum_scatter(
        lax.cond(is_student, product, nothing).astype(jnp.bfloat16),
        ("dp", "side"),
        scatter_dimension=0,
        tiled=True,
    ).astype(jnp.float32)

    def down_product():
        return lax.dot_general(
            hidden_act, grad_out, (((0,), (0,)), ((), ())), preferred_element_type=jnp.float32
        )

    def down_nothing():
        return jnp.zeros((ff_width, width), jnp.float32)

    down_term = lax.cond(is_student, down_product, down_nothing)
    down_share = lax.psum_scatter(
        down_term.astype(jnp.bfloat16), ("dp", "side"), scatter_dimension=1, tiled=True
    ).astype(jnp.float32)
    return (out_local[None], up_share, down_share)


def solution(mesh):
    placed = (
        P("dp", "mp"),
        P("side", "dp", "mp"),
        P("side", "mp", "dp"),
        P("side", None, None, None),
        P("dp"),
        P(),
    )
    return jax.shard_map(
        shards,
        mesh=mesh,
        in_specs=placed,
        out_specs=(P("side", "dp", "mp"), P(("dp", "side"), "mp"), P("mp", ("dp", "side"))),
        check_vma=False,
    )
```

profile of v0, /device:TPU:1, one launch (start us, length us, event | category | flops | bytes accessed | tf_op | source)
XLA Modules:
  0.0 593.4 jit_solution(2284106600337096998)
XLA Ops:
  9.4 6.5 %reduce = f32[50,3,3072]{2,1,0:T(4,128)S(1)} reduce(f32[1,50,3,3072]{3,0,2,1:T(1,128)} %param.15, f32[]{:T(128)} %constant.65), dimensions={0}, to_apply=%param.15.reduce_sub_computation | reduce | bytes 3686404 | tf_op args[3]
  16.5 1.2 copy.14
  19.1 29.2 %all-gather.6.cloned.1.call-done = bf16[256,3072]{1,0:T(8,128)(2,1)} async-done(((bf16[256,384]{1,0:T(8,128)(2,1)}), bf16[256,3072]{1,0:T(8,128)(2,1)}) %all-gather.6.cloned.1.call-update) | async-done | bytes 1572880 | tf_op jit(solution)/shard_map/all_gather | solution.py:18
  48.2 1.8 convert_reduce_fusion
  50.1 2.0 fusion.11
  52.8 41.7 %all-gather.8.cloned.1.call-done = bf16[1,3072,768]{2,1,0:T(8,128)(2,1)} async-done(((bf16[1,192,768]{2,1,0:T(8,128)(2,1)}), bf16[1,3072,768]{2,1,0:T(8,128)(2,1)}) %all-gather.8.cloned.1.call-update) | async-done | bytes 4718608 | tf_op jit(solution)/shard_map/all_gather | solution.py:40
  94.5 4.6 fusion.23
  99.2 37.7 %all-gather.10.cloned.1.call-done = bf16[1,768,3072]{1,2,0:T(8,128)(2,1)} async-done(((bf16[1,768,192]{1,2,0:T(8,128)(2,1)}), bf16[1,768,3072]{1,2,0:T(8,128)(2,1)}) %all-gather.10.cloned.1.call-update) | async-done | bytes 4718608 | tf_op jit(solution)/shard_map/all_gather | solution.py:44
  136.9 4.9 convolution_convert_fusion
  142.1 74.3 %all-reduce.2.cloned.1.call-done = bf16[256,3072]{1,0:T(8,128)(2,1)} async-done(((bf16[256,3072]{1,0:T(8,128)(2,1)}), bf16[256,3072]{1,0:T(8,128)(2,1)}) %all-reduce.2.cloned.1.call-update) | async-done | bytes 1572880 | tf_op jit(solution)/shard_map/psum | solution.py:50
  216.3 3.1 fusion.15
  219.5 5.8 collective-permute-start
  227.8 25.6 %collective-permute-done = bf16[256,3072]{1,0:T(8,128)(2,1)} collective-permute-done((bf16[256,3072]{1,0:T(8,128)(2,1)}, bf16[256,3072]{1,0:T(8,128)(2,1)}, u32[]{:S(2)}, u32[]{:S(2)}) %collective-permute-start) | collective-permute-done | bytes 1572896 | tf_op jit(solution)/shard_map/ppermute | solution.py:10
  253.4 2.6 divide_convert_fusion
  256.1 2.5 conditional.4
  256.1 2.5 broadcast.75
  259.6 2.8 conditional.5
  259.6 2.8 broadcast.76
  262.4 6.6 %copy.12 = bf16[768,3072]{0,1:T(8,128)(2,1)} copy(bf16[768,3072]{1,0:T(8,128)(2,1)} %get-tuple-element.43) | data formatting | bytes 9437184 | tf_op jit(solution)/shard_map/cond | solution.py:96
  269.0 1.6 dynamic-slice_bitcast_fusion
  270.6 155.2 %reduce-scatter.3.cloned.1.call-done = bf16[96,768]{1,0:T(8,128)(2,1)} async-done(((bf16[3072,768]{1,0:T(8,128)(2,1)}), bf16[96,768]{1,0:T(8,128)(2,1)}) %reduce-scatter.3.cloned.1.call-update) | async-done | bytes 147472 | tf_op jit(solution)/shard_map/reduce_scatter | solution.py:81
  425.9 1.6 convert_element_type.71
  427.5 157.4 %reduce-scatter.5.cloned.1.call-done = bf16[768,96]{0,1:T(8,128)(2,1)} async-done(((bf16[768,3072]{0,1:T(8,128)(2,1)}), bf16[768,96]{0,1:T(8,128)(2,1)}) %reduce-scatter.5.cloned.1.call-update) | async-done | bytes 147472 | tf_op jit(solution)/shard_map/reduce_scatter | solution.py:97
  584.9 1.6 convert_element_type.73
  (31 shorter events, 7.5 us)
Async XLA Ops:
  7.2 41.1 %all-gather.6.cloned.1.call-start = ((), (), s32[]{:S(2)}) async-start(), calls=%async_computation.2 | async-start | bytes 1769472 | tf_op jit(solution)/shard_map/all_gather | solution.py:18
  7.9 86.6 %all-gather.8.cloned.1.call-start = ((), (), s32[]{:S(2)}) async-start(), calls=%async_computation.6 | async-start | bytes 5013504 | tf_op jit(solution)/shard_map/all_gather | solution.py:40
  8.6 128.2 %all-gather.10.cloned.1.call-start = ((), (), s32[]{:S(2)}) async-start(), calls=%async_computation.7 | async-start | bytes 5013504 | tf_op jit(solution)/shard_map/all_gather | solution.py:44
  9.4 207.0 %all-reduce.2.cloned.1.call-start = ((), (), s32[]{:S(2)}) async-start(), calls=%async_computation.3 | async-start | bytes 3145728 | tf_op jit(solution)/shard_map/psum | solution.py:50
  48.2 3.8 copy-start
  99.2 42.7 %copy-start.1 = (bf16[256,768]{1,0:T(8,128)(2,1)}, bf16[256,768]{1,0:T(8,128)(2,1)S(1)}, u32[]{:S(2)}) copy-start(bf16[256,768]{1,0:T(8,128)(2,1)S(1)} %get-tuple-element.39) | copy-start | bytes 1179652
  141.8 83.4 %copy-start.3 = (s32[16]{0:T(128)S(1)}, s32[16]{0:T(128)}, u32[]{:S(2)}) copy-start(s32[16]{0:T(128)} %param.17) | copy-start | bytes 196
  141.8 284.0 %reduce-scatter.3.cloned.1.call-start = ((), (), s32[]{:S(2)}) async-start(), calls=%async_computation.4 | async-start | bytes 4866048 | tf_op jit(solution)/shard_map/reduce_scatter | solution.py:81
  219.5 34.0 %collective-permute-start = (bf16[256,3072]{1,0:T(8,128)(2,1)}, bf16[256,3072]{1,0:T(8,128)(2,1)}, u32[]{:S(2)}, u32[]{:S(2)}) collective-permute-start(bf16[256,3072]{1,0:T(8,128)(2,1)} %fusion.15), channel_id=1, source_target_pairs={{0,1},{2,3},{4,5},{6,7},{8,9},{10,11},{12,13},{14,15},{16,17},{18,... | collective-permute-start | bytes 4718600 | tf_op jit(solution)/shard_map/ppermute | solution.py:10
  258.6 1.0 copy-start.2
  258.6 326.3 %reduce-scatter.5.cloned.1.call-start = ((), (), s32[]{:S(2)}) async-start(), calls=%async_computation.5 | async-start | bytes 4866048 | tf_op jit(solution)/shard_map/reduce_scatter | solution.py:97
Sparse Core Ops, SparseCore 0:
  9.8 38.4 all-gather.5
  50.1 44.3 all-gather.7
  96.4 40.4 all-gather.9
  142.0 74.3 all-reduce.1
  258.7 167.0 reduce-scatter.2
  428.2 156.6 reduce-scatter.4
where the time goes:
time: 594 us; the launch traced here: 593 us
  waiting for transfers between devices  523 us (88%)
  other arithmetic  21.3 us (4%)
  local copies, waits for them, and re-layouts  16.8 us (3%)
  between operations  15.5 us (3%)
  matrix products  10.3 us (2%)
  starting transfers between devices  6.19 us (1%)
    reduce_scatter x1, waiting for transfers between devices, shards(): lax.psum_scatter(down_term.astype(jnp.bfloat16), ('dp', 'side'), scatter_...  157 us
    reduce_scatter x1, waiting for transfers between devices, shards(): lax.psum_scatter(lax.cond(is_student, product, nothing).astype(jnp.bfloat...  155 us
    psum x1, waiting for transfers between devices, shards(): lax.psum(partial_value.astype(jnp.bfloat16), 'mp').astype(jnp.float32)  74.3 us
    all_gather x1, waiting for transfers between devices, shards(): lax.all_gather(up_weight[0], 'dp', axis=0, tiled=True)  41.7 us
    all_gather x1, waiting for transfers between devices, shards(): down_full = lax.all_gather(down_weight[0], 'dp', axis=1, tiled=True)  37.7 us
    all_gather x1, waiting for transfers between devices, shards(): gathered = lax.all_gather(tokens, 'mp', axis=1, tiled=True)  29.2 us
    ppermute x1, waiting for transfers between devices, passed_along(): return lax.ppermute(x, axis, pairs)  25.6 us
  transfers between devices with their start and end apart: 7, of which 7 were waited for; matrix products, arithmetic and copies ran while one was open for 6% of the time, Pallas kernels for 0%

commit v1 on v0

--- a/solution.py
+++ b/solution.py
@@ -2,6 +2,11 @@
 import jax.numpy as jnp
 from jax import lax
 from jax.sharding import PartitionSpec as P
+
+
+def gather_blocks(x, axis, dim):
+    pieces = lax.all_gather(x, axis)
+    return jnp.concatenate(pieces, axis=dim)
 
 
 def passed_along(x, axis, by):
@@ -41,7 +46,7 @@
         preferred_element_type=jnp.float32,
     )
     hidden_act = gelu_tanh(hidden_pre).astype(jnp.bfloat16)
-    down_full = lax.all_gather(down_weight[0], "dp", axis=1, tiled=True)
+    down_full = gather_blocks(down_weight[0], "dp", 1)
     partial_value = jnp.dot(hidden_act, down_full, preferred_element_type=jnp.float32)
     positions = jnp.arange(normed.shape[0], dtype=jnp.int32)
     own_count = lax.dynamic_index_in_dim(valid_counts, lax.axis_index("dp"), 0, keepdims=False)

time: 594 us -> 594 us (level)
  no operation moved by 1% of the time
where the time goes in v1:
time: 594 us; the launch traced here: 593 us
  waiting for transfers between devices  523 us (88%)
  other arithmetic  21.3 us (4%)
  local copies, waits for them, and re-layouts  16.8 us (3%)
  between operations  15.5 us (3%)
  matrix products  10.3 us (2%)
  starting transfers between devices  6.19 us (1%)
    reduce_scatter x1, waiting for transfers between devices, shards(): lax.psum_scatter(down_term.astype(jnp.bfloat16), ('dp', 'side'), scatter_...  157 us
    reduce_scatter x1, waiting for transfers between devices, shards(): lax.psum_scatter(lax.cond(is_student, product, nothing).astype(jnp.bfloat...  155 us
    psum x1, waiting for transfers between devices, shards(): lax.psum(partial_value.astype(jnp.bfloat16), 'mp').astype(jnp.float32)  74.3 us
    all_gather x1, waiting for transfers between devices, shards(): lax.all_gather(up_weight[0], 'dp', axis=0, tiled=True)  41.7 us
    all_gather x1, waiting for transfers between devices, gather_blocks(): pieces = lax.all_gather(x, axis)  37.7 us
    all_gather x1, waiting for transfers between devices, shards(): gathered = lax.all_gather(tokens, 'mp', axis=1, tiled=True)  29.2 us
    ppermute x1, waiting for transfers between devices, passed_along(): return lax.ppermute(x, axis, pairs)  25.6 us
  transfers between devices with their start and end apart: 7, of which 7 were waited for; matrix products, arithmetic and copies ran while one was open for 6% of the time, Pallas kernels for 0%

profile of v1, /device:TPU:1, one launch (start us, length us, event | category | flops | bytes accessed | tf_op | source)
XLA Modules:
  0.0 593.4 jit_solution(2284106600337096998)
XLA Ops:
  9.4 6.5 %reduce = f32[50,3,3072]{2,1,0:T(4,128)S(1)} reduce(f32[1,50,3,3072]{3,0,2,1:T(1,128)} %param.15, f32[]{:T(128)} %constant.65), dimensions={0}, to_apply=%param.15.reduce_sub_computation | reduce | bytes 3686404 | tf_op args[3]
  16.5 1.2 copy.16
  19.1 29.2 %all-gather.5.cloned.1.call-done = bf16[256,3072]{1,0:T(8,128)(2,1)} async-done(((bf16[256,384]{1,0:T(8,128)(2,1)}), bf16[256,3072]{1,0:T(8,128)(2,1)}) %all-gather.5.cloned.1.call-update) | async-done | bytes 1572880 | tf_op jit(solution)/shard_map/all_gather | solution.py:23
  48.2 1.8 convert_reduce_fusion
  50.1 2.0 fusion.11
  52.8 41.7 %all-gather.9.cloned.1.call-done = bf16[1,3072,768]{2,1,0:T(8,128)(2,1)} async-done(((bf16[1,192,768]{2,1,0:T(8,128)(2,1)}), bf16[1,3072,768]{2,1,0:T(8,128)(2,1)}) %all-gather.9.cloned.1.call-update) | async-done | bytes 4718608 | tf_op jit(solution)/shard_map/all_gather | solution.py:45
  94.5 4.6 fusion.23
  99.2 37.7 %all-gather.7.cloned.1.call-done = bf16[16,768,192]{1,2,0:T(8,128)(2,1)} async-done(((bf16[1,768,192]{1,2,0:T(8,128)(2,1)}), bf16[16,768,192]{1,2,0:T(8,128)(2,1)}) %all-gather.7.cloned.1.call-update) | async-done | bytes 4718608 | tf_op jit(solution)/shard_map/all_gather | solution.py:8
  136.9 4.9 convolution_convert_fusion
  142.1 74.3 %all-reduce.2.cloned.1.call-done = bf16[256,3072]{1,0:T(8,128)(2,1)} async-done(((bf16[256,3072]{1,0:T(8,128)(2,1)}), bf16[256,3072]{1,0:T(8,128)(2,1)}) %all-reduce.2.cloned.1.call-update) | async-done | bytes 1572880 | tf_op jit(solution)/shard_map/psum | solution.py:55
  216.3 3.1 fusion.15
  219.5 5.8 collective-permute-start
  227.8 25.6 %collective-permute-done = bf16[256,3072]{1,0:T(8,128)(2,1)} collective-permute-done((bf16[256,3072]{1,0:T(8,128)(2,1)}, bf16[256,3072]{1,0:T(8,128)(2,1)}, u32[]{:S(2)}, u32[]{:S(2)}) %collective-permute-start) | collective-permute-done | bytes 1572896 | tf_op jit(solution)/shard_map/ppermute | solution.py:15
  253.4 2.6 divide_convert_fusion
  256.1 2.5 conditional.4
  256.1 2.5 broadcast.75
  259.6 2.8 conditional.5
  259.6 2.8 broadcast.76
  262.4 6.6 %copy.14 = bf16[768,3072]{0,1:T(8,128)(2,1)} copy(bf16[768,3072]{1,0:T(8,128)(2,1)} %get-tuple-element.46) | data formatting | bytes 9437184 | tf_op jit(solution)/shard_map/cond | solution.py:101
  269.0 1.6 dynamic-slice_bitcast_fusion
  270.6 155.2 %reduce-scatter.3.cloned.1.call-done = bf16[96,768]{1,0:T(8,128)(2,1)} async-done(((bf16[3072,768]{1,0:T(8,128)(2,1)}), bf16[96,768]{1,0:T(8,128)(2,1)}) %reduce-scatter.3.cloned.1.call-update) | async-done | bytes 147472 | tf_op jit(solution)/shard_map/reduce_scatter | solution.py:86
  425.9 1.6 convert_element_type.71
  427.5 157.4 %reduce-scatter.5.cloned.1.call-done = bf16[768,96]{0,1:T(8,128)(2,1)} async-done(((bf16[768,3072]{0,1:T(8,128)(2,1)}), bf16[768,96]{0,1:T(8,128)(2,1)}) %reduce-scatter.5.cloned.1.call-update) | async-done | bytes 147472 | tf_op jit(solution)/shard_map/reduce_scatter | solution.py:102
  584.9 1.6 convert_element_type.73
  (31 shorter events, 7.5 us)
Async XLA Ops:
  7.2 41.1 %all-gather.5.cloned.1.call-start = ((), (), s32[]{:S(2)}) async-start(), calls=%async_computation.2 | async-start | bytes 1769472 | tf_op jit(solution)/shard_map/all_gather | solution.py:23
  7.9 86.6 %all-gather.9.cloned.1.call-start = ((), (), s32[]{:S(2)}) async-start(), calls=%async_computation.7 | async-start | bytes 5013504 | tf_op jit(solution)/shard_map/all_gather | solution.py:45
  8.6 128.2 %all-gather.7.cloned.1.call-start = ((), (), s32[]{:S(2)}) async-start(), calls=%async_computation.3 | async-start | bytes 5013504 | tf_op jit(solution)/shard_map/all_gather | solution.py:8
  9.4 207.0 %all-reduce.2.cloned.1.call-start = ((), (), s32[]{:S(2)}) async-start(), calls=%async_computation.4 | async-start | bytes 3145728 | tf_op jit(solution)/shard_map/psum | solution.py:55
  48.2 3.8 copy-start
  99.2 42.7 %copy-start.1 = (bf16[256,768]{1,0:T(8,128)(2,1)}, bf16[256,768]{1,0:T(8,128)(2,1)S(1)}, u32[]{:S(2)}) copy-start(bf16[256,768]{1,0:T(8,128)(2,1)S(1)} %get-tuple-element.42) | copy-start | bytes 1179652
  141.8 83.4 %copy-start.3 = (s32[16]{0:T(128)S(1)}, s32[16]{0:T(128)}, u32[]{:S(2)}) copy-start(s32[16]{0:T(128)} %param.17) | copy-start | bytes 196
  141.8 284.0 %reduce-scatter.3.cloned.1.call-start = ((), (), s32[]{:S(2)}) async-start(), calls=%async_computation.5 | async-start | bytes 4866048 | tf_op jit(solution)/shard_map/reduce_scatter | solution.py:86
  219.5 34.0 %collective-permute-start = (bf16[256,3072]{1,0:T(8,128)(2,1)}, bf16[256,3072]{1,0:T(8,128)(2,1)}, u32[]{:S(2)}, u32[]{:S(2)}) collective-permute-start(bf16[256,3072]{1,0:T(8,128)(2,1)} %fusion.15), channel_id=1, source_target_pairs={{0,1},{2,3},{4,5},{6,7},{8,9},{10,11},{12,13},{14,15},{16,17},{18,... | collective-permute-start | bytes 4718600 | tf_op jit(solution)/shard_map/ppermute | solution.py:15
  258.6 1.0 copy-start.2
  258.6 326.3 %reduce-scatter.5.cloned.1.call-start = ((), (), s32[]{:S(2)}) async-start(), calls=%async_computation.6 | async-start | bytes 4866048 | tf_op jit(solution)/shard_map/reduce_scatter | solution.py:102
Sparse Core Ops, SparseCore 0:
  9.8 38.4 all-gather.4
  50.1 44.3 all-gather.8
  96.4 40.4 all-gather.6
  142.0 74.3 all-reduce.1
  258.7 167.0 reduce-scatter.2
  428.2 156.6 reduce-scatter.4
